TPU v7x, 256 devices: a whole 4x4x8 slice. The times are simulated.
256 devices in a mesh: branch: 2 (over core), gi: 16 (over y_hi, z), gj: 8 (over x, y_lo).
Axes of the slice: x: 4, y: 4 (y_hi: 2, y_lo: 2; y = y_hi * 2 + y_lo), z: 8, core: 2. Of those that a mesh axis runs over, the one named last changes fastest.
Arguments:
- homolog_embedding: float32 [128, 256, 256], P(('branch', 'gj'), 'gi'), may hold values from -6 to 6
- pair_input_tensor: float32 [256, 256, 128], P('gi', ('branch', 'gj')), may hold values from -6 to 6
- layernorm_scales: float32 [4, 256], replicated, may hold values from 0.5 to 1.5
- pair_norm_gains: float32 [3, 128], replicated, may hold values from 0.5 to 1.5
- pair_bias_matrix: float32 [128, 8], replicated
- horizontal_qkvg_kernel: float32 [256, 1024], replicated, may hold values from -0.375 to 0.375
- horizontal_final_kernel: float32 [256, 256], replicated, may hold values from -0.375 to 0.375
- vertical_qkvg_kernel: float32 [256, 1024], replicated, may hold values from -0.375 to 0.375
- vertical_final_kernel: float32 [256, 256], replicated, may hold values from -0.375 to 0.375
- feedforward_expand_kernel: float32 [256, 1024], replicated, may hold values from -0.375 to 0.375
- feedforward_shrink_kernel: float32 [1024, 256], replicated, may hold values from -0.1875 to 0.1875
- dyadic_sides_kernel: float32 [256, 64], replicated, may hold values from -0.375 to 0.375
- outer_output_matrix: float32 [1024, 128], replicated, may hold values from -1 to 1
- triangle_input_matrix: float32 [128, 640], replicated, may hold values from -0.5 to 0.5
- triangle_output_matrix: float32 [128, 128], replicated, may hold values from -0.5 to 0.5
Outputs:
- alignment_output: float32 [128, 256, 256], P(('branch', 'gj'), 'gi')
- pair_output_tensor: float32 [256, 256, 128], P('gi', ('branch', 'gj'))
All inputs are finite; a program needn't handle non-finite values.
Results may differ from a plain program's by a relative error of at most 0.0003.
Values sent between devices are 32-bit elements; how exact they have to be, the bound alone decides.
A program may use at most 64 MiB of HBM per device.

v0:
```python
import math
import jax
import jax.numpy as jnp
from jax import lax
from jax.sharding import PartitionSpec as P

epsilon = 1e-05
highest = lax.Precision.HIGHEST
lowest_start = -1e30


def from_root(shard, axis, root):
    mine = lax.axis_index(axis) == root
    return lax.psum(jnp.where(mine, shard, jnp.zeros_like(shard)), axis)


def layer_normalise(values, norm_gain):
    average = jnp.mean(values, axis=-1, keepdims=True)
    centred = values - average
    variance = jnp.mean(centred * centred, axis=-1, keepdims=True)
    return centred * lax.rsqrt(variance + epsilon) * norm_gain


def apply_projection(values, weight):
    return jnp.einsum("...c,cd->...d", values, weight, precision=highest)


def transition_update(values, norm_gain, feedforward_expand_kernel, feedforward_shrink_kernel):
    expanded = jax.nn.relu(
        apply_projection(layer_normalise(values, norm_gain), feedforward_expand_kernel)
    )
    return values + apply_projection(expanded, feedforward_shrink_kernel)


def online_update(state_carry, scores, values, einsum_form):
    running_max, sum_weights, numerator = state_carry
    new_max = jnp.maximum(running_max, jnp.max(scores, axis=-1))
    weights = jnp.exp(scores - new_max[..., None])
    sum_weights = jnp.sum(weights, axis=-1)
    numerator = jnp.einsum(einsum_form, weights, values, precision=highest)
    return (new_max, sum_weights, numerator)


def empty_state(leading, head_size):
    return (
        jnp.full(leading, lowest_start, jnp.float32),
        jnp.zeros(leading, jnp.float32),
        jnp.zeros(leading + (head_size,), jnp.float32),
    )


def panels(first_local, second_local):
    groups = lax.axis_size("gi") // lax.axis_size(("branch", "gj"))
    col_index = lax.axis_index(("branch", "gj"))
    first_panel, second_panel = (
        lax.all_gather(first_local, ("branch", "gj"), axis=1, tiled=True),
        lax.all_gather(second_local, ("branch", "gj"), axis=1, tiled=True),
    )
    pieces = from_root(second_panel, "gi", col_index * groups + 0)
    return (first_panel, pieces)


def per_device(
    homolog_embedding,
    pair_input_tensor,
    layernorm_scales,
    pair_norm_gains,
    pair_bias_matrix,
    horizontal_qkvg_kernel,
    horizontal_final_kernel,
    vertical_qkvg_kernel,
    vertical_final_kernel,
    feedforward_expand_kernel,
    feedforward_shrink_kernel,
    dyadic_sides_kernel,
    outer_output_matrix,
    triangle_input_matrix,
    triangle_output_matrix,
):
    rows_per_device, residues_per_device, alignment_width = homolog_embedding.shape
    pair_cols, pair_width = (pair_input_tensor.shape[1], pair_input_tensor.shape[2])
    head_count = pair_bias_matrix.shape[1]
    inner_feature_width = horizontal_final_kernel.shape[0]
    head_size = inner_feature_width // head_count
    outer_width = dyadic_sides_kernel.shape[1] // 2
    bias_local = apply_projection(
        layer_normalise(pair_input_tensor, pair_norm_gains[0]), pair_bias_matrix
    ).reshape(residues_per_device, pair_cols * head_count)
    bias_rows = lax.all_gather(bias_local, ("branch", "gj"), axis=1, tiled=True).reshape(
        residues_per_device, -1, head_count
    )
    bias_heads = jnp.transpose(bias_rows, (2, 0, 1))
    alignment_normalised = layer_normalise(homolog_embedding, layernorm_scales[0])
    row_query_values = apply_projection(
        alignment_normalised, horizontal_qkvg_kernel[:, :inner_feature_width]
    ).reshape(rows_per_device, residues_per_device, head_count, head_size)
    row_gate_values = apply_projection(
        alignment_normalised, horizontal_qkvg_kernel[:, 3 * inner_feature_width :]
    )
    row_start = empty_state((rows_per_device, head_count, residues_per_device), head_size)
    row_pair_slice = apply_projection(
        alignment_normalised,
        horizontal_qkvg_kernel[:, inner_feature_width : 3 * inner_feature_width],
    )
    pieces = (
        lax.all_gather(row_pair_slice[..., :inner_feature_width], "gi", axis=1, tiled=True),
        lax.all_gather(row_pair_slice[..., inner_feature_width:], "gi", axis=1, tiled=True),
    )
    key_flat = pieces[0]
    block_rows = key_flat.shape[1]
    key_block = key_flat.reshape(rows_per_device, block_rows, head_count, head_size)
    value_block = pieces[1].reshape(rows_per_device, block_rows, head_count, head_size)
    scores = (
        jnp.einsum("sihd,sjhd->shij", row_query_values, key_block, precision=highest)
        / math.sqrt(head_size)
        + bias_heads[None]
    )
    row_state = online_update(row_start, scores, value_block, "shij,sjhd->shid")
    row_heads = row_state[2] / row_state[1][..., None]
    row_attention_result = jnp.transpose(row_heads, (0, 2, 1, 3)).reshape(
        rows_per_device, residues_per_device, inner_feature_width
    )
    alignment_after_rows = homolog_embedding + apply_projection(
        jax.nn.sigmoid(row_gate_values) * row_attention_result, horizontal_final_kernel
    )
    column_normalised = layer_normalise(alignment_after_rows, layernorm_scales[1])
    column_query = apply_projection(
        column_normalised, vertical_qkvg_kernel[:, :inner_feature_width]
    ).reshape(rows_per_device, residues_per_device, head_count, head_size)
    column_pairs = apply_projection(
        column_normalised, vertical_qkvg_kernel[:, inner_feature_width : 3 * inner_feature_width]
    )
    column_gate_values = apply_projection(
        column_normalised, vertical_qkvg_kernel[:, 3 * inner_feature_width :]
    )
    column_start = empty_state((residues_per_device, head_count, rows_per_device), head_size)
    pieces = (
        lax.all_gather(
            column_pairs[..., :inner_feature_width], ("branch", "gj"), axis=0, tiled=True
        ),
        lax.all_gather(
            column_pairs[..., inner_feature_width:], ("branch", "gj"), axis=0, tiled=True
        ),
    )
    block_rows = pieces[0].shape[0]
    key_block = pieces[0].reshape(block_rows, residues_per_device, head_count, head_size)
    value_block = pieces[1].reshape(block_rows, residues_per_device, head_count, head_size)
    scores = jnp.einsum("sihd,tihd->ihst", column_query, key_block, precision=highest) / math.sqrt(
        head_size
    )
    column_state = online_update(column_start, scores, value_block, "ihst,tihd->ihsd")
    column_heads = column_state[2] / column_state[1][..., None]
    column_attention_result = jnp.transpose(column_heads, (2, 0, 1, 3)).reshape(
        rows_per_device, residues_per_device, inner_feature_width
    )
    alignment_after_columns = alignment_after_rows + apply_projection(
        jax.nn.sigmoid(column_gate_values) * column_attention_result, vertical_final_kernel
    )
    alignment_output = transition_update(
        alignment_after_columns,
        layernorm_scales[2],
        feedforward_expand_kernel,
        feedforward_shrink_kernel,
    )
    factor_pair = apply_projection(
        layer_normalise(alignment_output, layernorm_scales[3]), dyadic_sides_kernel
    )
    left_local = jnp.transpose(factor_pair[..., :outer_width], (1, 0, 2)).reshape(
        residues_per_device, rows_per_device * outer_width
    )
    right_local = jnp.transpose(factor_pair[..., outer_width:], (1, 0, 2)).reshape(
        residues_per_device, rows_per_device * outer_width
    )
    left_panel, right_panel = panels(left_local, right_local)
    all_rows = left_panel.shape[1] // outer_width
    left_three = left_panel.reshape(residues_per_device, all_rows, outer_width)
    right_three = right_panel.reshape(pair_cols, all_rows, outer_width)
    outer = jnp.einsum("isc,jsd->ijcd", left_three, right_three, precision=highest) / all_rows
    pair_first = pair_input_tensor + apply_projection(
        outer.reshape(residues_per_device, pair_cols, outer_width * outer_width),
        outer_output_matrix,
    )
    projected_values = apply_projection(
        layer_normalise(pair_first, pair_norm_gains[1]), triangle_input_matrix
    )
    left_tri = (
        jax.nn.sigmoid(projected_values[..., pair_width : 2 * pair_width])
        * projected_values[..., :pair_width]
    )
    right_tri = (
        jax.nn.sigmoid(projected_values[..., 3 * pair_width : 4 * pair_width])
        * projected_values[..., 2 * pair_width : 3 * pair_width]
    )
    out_gate = projected_values[..., 4 * pair_width :]
    left_rows, right_rows = panels(
        left_tri.reshape(residues_per_device, pair_cols * pair_width),
        right_tri.reshape(residues_per_device, pair_cols * pair_width),
    )
    left_rows = left_rows.reshape(residues_per_device, -1, pair_width)
    right_rows = right_rows.reshape(pair_cols, -1, pair_width)
    product = jnp.einsum("ikc,jkc->ijc", left_rows, right_rows, precision=highest)
    pair_output_tensor = pair_first + jax.nn.sigmoid(out_gate) * apply_projection(
        layer_normalise(product, pair_norm_gains[2]), triangle_output_matrix
    )
    return (alignment_output, pair_output_tensor)


def solution(mesh):
    return jax.shard_map(
        per_device,
        mesh=mesh,
        in_specs=(
            P(("branch", "gj"), "gi", None),
            P("gi", ("branch", "gj"), None),
            P(),
            P(),
            P(),
            P(),
            P(),
            P(),
            P(),
            P(),
            P(),
            P(),
            P(),
            P(),
            P(),
        ),
        out_specs=(P(("branch", "gj"), "gi", None), P("gi", ("branch", "gj"), None)),
        check_vma=False,
    )
```

profile of v0, /device:TPU:2, one launch (start us, length us, event | category | flops | bytes accessed | tf_op | source)
XLA Modules:
  0.0 740.1 jit_solution(3773819482061920002)
XLA Ops:
  9.5 1.4 fusion.100
  10.8 1.6 fusion.19
  17.5 40.2 %all_gather.28 = f32[16,2048]{0,1:T(8,128)S(1)} all-gather(f32[16,128]{0,1:T(8,128)S(1)} %convolution_bitcast_fusion.2), channel_id=1, replica_groups=mesh['branch'=2,'gi'=16,'gj'=8] {'branch','gj'}, dimensions={1}, use_global_device_ids=true | all-gather | bytes 139264 | tf_op jit(solution)/shard_map/all_gather | solution.py:89
  58.1 44.4 %all-gather.7.cloned.1.call-done = f32[8,256,256]{2,1,0:T(8,128)} async-done(((f32[8,16,256]{2,1,0:T(8,128)}), f32[8,256,256]{2,1,0:T(8,128)}) %all-gather.7.cloned.1.call-update) | async-done | bytes 2097168 | tf_op jit(solution)/shard_map/all_gather | solution.py:106
  102.4 2.9 copy.90
  105.4 2.9 fusion.101
  108.7 79.0 %all-gather.9.cloned.1.call-done = f32[8,256,256]{2,1,0:T(8,128)} async-done(((f32[8,16,256]{2,1,0:T(8,128)}), f32[8,256,256]{2,1,0:T(8,128)}) %all-gather.9.cloned.1.call-update) | async-done | bytes 2097168 | tf_op jit(solution)/shard_map/all_gather | solution.py:107
  187.7 2.9 copy.94
  190.6 3.5 fusion.1
  195.9 1.3 fusion.102
  200.7 30.8 %all-gather.11.cloned.1.call-done = f32[128,16,256]{2,1,0:T(8,128)} async-done(((f32[8,16,256]{2,1,0:T(8,128)}), f32[128,16,256]{2,1,0:T(8,128)}) %all-gather.11.cloned.1.call-update) | async-done | bytes 2097168 | tf_op jit(solution)/shard_map/all_gather | solution.py:138
  231.4 2.0 copy.96
  233.4 3.2 fusion.103
  237.8 32.4 %all-gather.13.cloned.1.call-done = f32[128,16,256]{2,1,0:T(8,128)} async-done(((f32[8,16,256]{2,1,0:T(8,128)}), f32[128,16,256]{2,1,0:T(8,128)}) %all-gather.13.cloned.1.call-update) | async-done | bytes 2097168 | tf_op jit(solution)/shard_map/all_gather | solution.py:141
  270.2 2.0 copy.98
  272.2 4.5 fusion.2
  277.0 1.6 fusion.6
  281.4 28.4 %all_gather.32 = f32[16,4096]{1,0:T(8,128)S(1)} all-gather(f32[16,256]{1,0:T(8,128)S(1)} %reshape.171), channel_id=1, replica_groups=mesh['branch'=2,'gi'=16,'gj'=8] {'branch','gj'}, dimensions={1}, use_global_device_ids=true | all-gather | bytes 278528 | tf_op jit(solution)/shard_map/all_gather | solution.py:57
  311.3 28.2 %all_gather.33 = f32[16,4096]{1,0:T(8,128)S(1)} all-gather(f32[16,256]{1,0:T(8,128)S(1)} %reshape.173), channel_id=1, replica_groups=mesh['branch'=2,'gi'=16,'gj'=8] {'branch','gj'}, dimensions={1}, use_global_device_ids=true | all-gather | bytes 278528 | tf_op jit(solution)/shard_map/all_gather | solution.py:56
  339.8 128.2 %all-reduce.3.cloned.1.call-done = f32[16,128,32]{1,2,0:T(8,128)} async-done(((f32[16,128,32]{1,2,0:T(8,128)}), f32[16,128,32]{1,2,0:T(8,128)}) %all-reduce.3.cloned.1.call-update) | async-done | bytes 262160 | tf_op jit(solution)/shard_map/psum | solution.py:14
  468.1 5.9 multiply_bitcast_fusion
  473.9 5.4 copy.104
  479.3 3.8 reshape.175
  487.7 32.8 %all-gather.15.cloned.1.call-done = f32[16,32768]{1,0:T(8,128)} async-done(((f32[16,2048]{1,0:T(8,128)}), f32[16,32768]{1,0:T(8,128)}) %all-gather.15.cloned.1.call-update) | async-done | bytes 2097168 | tf_op jit(solution)/shard_map/all_gather | solution.py:57
  521.0 2.1 copy.105
  523.1 35.6 %all-gather.17.cloned.1.call-done = f32[16,32768]{1,0:T(8,128)} async-done(((f32[16,2048]{1,0:T(8,128)}), f32[16,32768]{1,0:T(8,128)}) %all-gather.17.cloned.1.call-update) | async-done | bytes 2097168 | tf_op jit(solution)/shard_map/all_gather | solution.py:56
  558.7 3.3 copy.122
  562.1 2.2 copy.106
  564.4 160.5 %all-reduce.5.cloned.1.call-done = f32[16,256,128]{1,0,2:T(8,128)} async-done(((f32[16,256,128]{1,0,2:T(8,128)}), f32[16,256,128]{1,0,2:T(8,128)}) %all-reduce.5.cloned.1.call-update) | async-done | bytes 2097168 | tf_op jit(solution)/shard_map/psum | solution.py:14
  724.8 4.6 bitcast_reduce_fusion
  729.5 1.6 copy.107
  731.4 1.9 fusion.11
  (116 shorter events, 24.4 us)
Async XLA Ops:
  7.2 272.0 %copy-start = (f32[256,1024]{1,0:T(8,128)S(1)}, f32[256,1024]{1,0:T(8,128)}, u32[]{:S(2)}) copy-start(f32[256,1024]{1,0:T(8,128)} %param.24) | copy-start | bytes 3145732
  7.2 6.9 copy-start.2
  7.2 6.7 copy-start.4
  7.2 8.5 %copy-start.15 = (f32[3,128]{1,0:T(4,128)S(1)}, f32[3,128]{1,0:T(4,128)}, u32[]{:S(2)}) copy-start(f32[3,128]{1,0:T(4,128)} %param.18) | copy-start | bytes 4612
  7.2 9.3 %copy-start.13 = (f32[128,8]{0,1:T(8,128)S(1)}, f32[128,8]{0,1:T(8,128)}, u32[]{:S(2)}) copy-start(f32[128,8]{0,1:T(8,128)} %param.19) | copy-start | bytes 12292
  7.2 95.2 %all-gather.7.cloned.1.call-start = ((), (), s32[]{:S(2)}) async-start(), calls=%async_computation | async-start | bytes 2228224 | tf_op jit(solution)/shard_map/all_gather | solution.py:106
  13.1 174.6 %all-gather.9.cloned.1.call-start = ((), (), s32[]{:S(2)}) async-start(), calls=%async_computation.1 | async-start | bytes 2228224 | tf_op jit(solution)/shard_map/all_gather | solution.py:107
  13.9 217.6 %all-gather.11.cloned.1.call-start = ((), (), s32[]{:S(2)}) async-start(), calls=%async_computation.2 | async-start | bytes 2228224 | tf_op jit(solution)/shard_map/all_gather | solution.py:138
  194.2 3.2 copy-start.7
  198.6 71.6 %all-gather.13.cloned.1.call-start = ((), (), s32[]{:S(2)}) async-start(), calls=%async_computation.3 | async-start | bytes 2228224 | tf_op jit(solution)/shard_map/all_gather | solution.py:141
  199.2 268.9 %all-reduce.3.cloned.1.call-start = ((), (), s32[]{:S(2)}) async-start(), calls=%async_computation.4 | async-start | bytes 524288 | tf_op jit(solution)/shard_map/psum | solution.py:14
  236.6 0.8 copy-start.1
  276.6 1.9 copy-start.10
  276.6 2.5 copy-start.12
  276.8 3.1 copy-start.6
  278.9 1.9 copy-start.11
  280.6 30.5 %copy-start.5 = (f32[8,16,256]{2,1,0:T(8,128)}, f32[8,16,256]{2,1,0:T(8,128)S(1)}, u32[]{:S(2)}) copy-start(f32[8,16,256]{2,1,0:T(8,128)S(1)} %get-tuple-element.26) | copy-start | bytes 393220
  311.1 209.3 %all-gather.15.cloned.1.call-start = ((), (), s32[]{:S(2)}) async-start(), calls=%async_computation.5 | async-start | bytes 2228224 | tf_op jit(solution)/shard_map/all_gather | solution.py:57
  479.3 3.8 copy-start.8
  479.3 5.1 copy-start.14
  483.1 1.3 copy-start.9
  485.2 0.9 copy-start.3
  486.9 71.9 %all-gather.17.cloned.1.call-start = ((), (), s32[]{:S(2)}) async-start(), calls=%async_computation.7 | async-start | bytes 2228224 | tf_op jit(solution)/shard_map/all_gather | solution.py:56
  487.6 237.2 %all-reduce.5.cloned.1.call-start = ((), (), s32[]{:S(2)}) async-start(), calls=%async_computation.6 | async-start | bytes 4194304 | tf_op jit(solution)/shard_map/psum | solution.py:14
  564.3 167.1 %copy-start.16 = (f32[128]{0:T(128)S(1)}, f32[128]{0:T(128)}, u32[]{:S(2)}) copy-start(f32[128]{0:T(128)} %get-tuple-element.14) | copy-start | bytes 1540
  564.3 167.1 %copy-start.17 = (f32[128,128]{1,0:T(8,128)S(1)}, f32[128,128]{1,0:T(8,128)}, u32[]{:S(2)}) copy-start(f32[128,128]{1,0:T(8,128)} %param.29) | copy-start | bytes 196612
Sparse Core Ops, SparseCore 0:
  13.3 89.1 all-gather.6
  105.6 82.0 all-gather.8
  198.7 32.7 all-gather.10
  233.7 36.3 all-gather.12
  311.2 156.7 all-reduce.2
  487.0 33.4 all-gather.14
  522.3 36.3 all-gather.16
  561.4 163.4 all-reduce.4
where the time goes:
time: 741 us; the launch traced here: 740 us
  waiting for transfers between devices  545 us (74%)
  blocking collectives  96.8 us (13%)
  local copies, waits for them, and re-layouts  39.3 us (5%)
  matrix products  39.2 us (5%)
  between operations  14.8 us (2%)
    psum x2, waiting for transfers between devices, from_root(): return lax.psum(jnp.where(mine, shard, jnp.zeros_like(shard)), axis)  289 us
    all_gather x1, waiting for transfers between devices, per_device(): lax.all_gather(row_pair_slice[..., inner_feature_width:], 'gi', axis=1, t...  79 us
    all_gather x1, waiting for transfers between devices, per_device(): lax.all_gather(row_pair_slice[..., :inner_feature_width], 'gi', axis=1, t...  44.4 us
    all_gather x1, blocking collectives, per_device(): lax.all_gather(bias_local, ('branch', 'gj'), axis=1, tiled=True)  40.2 us
    all_gather x1, waiting for transfers between devices, panels(): lax.all_gather(first_local, ('branch', 'gj'), axis=1, tiled=True)  35.6 us
    all_gather x1, waiting for transfers between devices, panels(): lax.all_gather(second_local, ('branch', 'gj'), axis=1, tiled=True)  32.8 us
    all_gather x1, waiting for transfers between devices, per_device(): lax.all_gather(column_pairs[..., inner_feature_width:], ('branch', 'gj'),...  32.4 us
    all_gather x1, waiting for transfers between devices, per_device(): lax.all_gather(column_pairs[..., :inner_feature_width], ('branch', 'gj'),...  30.8 us
  transfers between devices with their start and end apart: 8, of which 8 were waited for; matrix products, arithmetic and copies ran while one was open for 4% of the time, Pallas kernels for 0%

commit v1 on v0

--- a/solution.py
+++ b/solution.py
@@ -7,11 +7,12 @@
 epsilon = 1e-05
 highest = lax.Precision.HIGHEST
 lowest_start = -1e30
+fit_plate = lambda mine_x, mesh_ax: jnp.sum(lax.all_gather(mine_x, axis_name=mesh_ax), axis=0)
 
 
 def from_root(shard, axis, root):
     mine = lax.axis_index(axis) == root
-    return lax.psum(jnp.where(mine, shard, jnp.zeros_like(shard)), axis)
+    return fit_plate(jnp.where(mine, shard, jnp.zeros_like(shard)), axis)
 
 
 def layer_normalise(values, norm_gain):

time: 741 us -> 953 us (1.29)
  waiting for transfers between devices: 545 us -> 737 us
  other arithmetic: 4.57 us -> 22 us
    all_gather x0 -> x2, waiting for transfers between devices: none -> 481 us  [lax.all_gather(mine_x, axis_name=mesh_ax)]
    psum x2 -> x0, waiting for transfers between devices: 289 us -> none  [from_root(): return lax.psum(jnp.where(mine, shard, jnp.zeros_like(shard)), axis)]
    reduce_sum x0 -> x2, other arithmetic: none -> 15.4 us  [jnp.sum(lax.all_gather(mine_x, axis_name=mesh_ax), axis=0)]
  transfers between devices with their start and end apart: 8 -> 8, of which waited for: 8 -> 8; matrix products, arithmetic and copies ran while one was open for 4% -> 3% of each run, Pallas kernels for 0% -> 0%
where the time goes in v1:
time: 953 us; the launch traced here: 952 us
  waiting for transfers between devices  737 us (77%)
  blocking collectives  97 us (10%)
  local copies, waits for them, and re-layouts  41.4 us (4%)
  matrix products  38.6 us (4%)
  other arithmetic  22 us (2%)
  between operations  14.8 us (2%)
    all_gather x2, waiting for transfers between devices, lax.all_gather(mine_x, axis_name=mesh_ax)  481 us
    all_gather x1, waiting for transfers between devices, per_device(): lax.all_gather(row_pair_slice[..., inner_feature_width:], 'gi', axis=1, t...  79 us
    all_gather x1, waiting for transfers between devices, per_device(): lax.all_gather(row_pair_slice[..., :inner_feature_width], 'gi', axis=1, t...  44.3 us
    all_gather x1, blocking collectives, per_device(): lax.all_gather(bias_local, ('branch', 'gj'), axis=1, tiled=True)  40.3 us
    all_gather x1, waiting for transfers between devices, panels(): lax.all_gather(first_local, ('branch', 'gj'), axis=1, tiled=True)  36.8 us
    all_gather x1, waiting for transfers between devices, per_device(): lax.all_gather(column_pairs[..., inner_feature_width:], ('branch', 'gj'),...  32.4 us
    all_gather x1, waiting for transfers between devices, panels(): lax.all_gather(second_local, ('branch', 'gj'), axis=1, tiled=True)  31.9 us
    all_gather x1, waiting for transfers between devices, per_device(): lax.all_gather(column_pairs[..., :inner_feature_width], ('branch', 'gj'),...  30.8 us
  transfers between devices with their start and end apart: 8, of which 8 were waited for; matrix products, arithmetic and copies ran while one was open for 3% of the time, Pallas kernels for 0%

profile of v1, /device:TPU:2, one launch (start us, length us, event | category | flops | bytes accessed | tf_op | source)
XLA Modules:
  0.0 951.7 jit_solution(2299638661625144908)
XLA Ops:
  17.5 40.3 %all_gather.40 = f32[16,2048]{0,1:T(8,128)S(1)} all-gather(f32[16,128]{0,1:T(8,128)S(1)} %convolution_bitcast_fusion.2), channel_id=1, replica_groups=mesh['branch'=2,'gi'=16,'gj'=8] {'branch','gj'}, dimensions={1}, use_global_device_ids=true | all-gather | bytes 139264 | tf_op jit(solution)/shard_map/all_gather | solution.py:90
  58.2 44.3 %all-gather.11.cloned.1.call-done = f32[8,256,256]{2,1,0:T(8,128)} async-done(((f32[8,16,256]{2,1,0:T(8,128)}), f32[8,256,256]{2,1,0:T(8,128)}) %all-gather.11.cloned.1.call-update) | async-done | bytes 2097168 | tf_op jit(solution)/shard_map/all_gather | solution.py:107
  102.5 2.9 copy.90
  105.4 2.9 fusion.101
  108.7 79.0 %all-gather.13.cloned.1.call-done = f32[8,256,256]{2,1,0:T(8,128)} async-done(((f32[8,16,256]{2,1,0:T(8,128)}), f32[8,256,256]{2,1,0:T(8,128)}) %all-gather.13.cloned.1.call-update) | async-done | bytes 2097168 | tf_op jit(solution)/shard_map/all_gather | solution.py:108
  187.8 2.9 copy.94
  190.6 3.5 fusion.1
  200.7 30.8 %all-gather.15.cloned.1.call-done = f32[128,16,256]{2,1,0:T(8,128)} async-done(((f32[8,16,256]{2,1,0:T(8,128)}), f32[128,16,256]{2,1,0:T(8,128)}) %all-gather.15.cloned.1.call-update) | async-done | bytes 2097168 | tf_op jit(solution)/shard_map/all_gather | solution.py:139
  231.5 2.0 copy.96
  233.5 3.2 fusion.103
  237.8 32.4 %all-gather.17.cloned.1.call-done = f32[128,16,256]{2,1,0:T(8,128)} async-done(((f32[8,16,256]{2,1,0:T(8,128)}), f32[128,16,256]{2,1,0:T(8,128)}) %all-gather.17.cloned.1.call-update) | async-done | bytes 2097168 | tf_op jit(solution)/shard_map/all_gather | solution.py:142
  270.2 2.0 copy.98
  272.2 4.5 fusion.2
  277.0 1.6 fusion.6
  281.4 28.4 %all_gather.44 = f32[16,4096]{1,0:T(8,128)S(1)} all-gather(f32[16,256]{1,0:T(8,128)S(1)} %reshape.171), channel_id=1, replica_groups=mesh['branch'=2,'gi'=16,'gj'=8] {'branch','gj'}, dimensions={1}, use_global_device_ids=true | all-gather | bytes 278528 | tf_op jit(solution)/shard_map/all_gather | solution.py:58
  310.6 28.3 %all_gather.47 = f32[16,4096]{1,0:T(8,128)S(1)} all-gather(f32[16,256]{1,0:T(8,128)S(1)} %reshape.173), channel_id=1, replica_groups=mesh['branch'=2,'gi'=16,'gj'=8] {'branch','gj'}, dimensions={1}, use_global_device_ids=true | all-gather | bytes 278528 | tf_op jit(solution)/shard_map/all_gather | solution.py:57
  339.3 70.8 %all-gather.23.cloned.1.call-done = f32[256,4096]{1,0:T(8,128)} async-done(((f32[16,4096]{1,0:T(8,128)}), f32[256,4096]{1,0:T(8,128)}) %all-gather.23.cloned.1.call-update) | async-done | bytes 4194320 | tf_op jit(solution)/shard_map/all_gather | solution.py:10
  410.1 2.4 reduce_sum.174
  412.9 5.2 multiply_bitcast_fusion
  418.1 5.4 copy.104
  423.4 3.8 reshape.175
  431.0 31.9 %all-gather.19.cloned.1.call-done = f32[16,32768]{1,0:T(8,128)} async-done(((f32[16,2048]{1,0:T(8,128)}), f32[16,32768]{1,0:T(8,128)}) %all-gather.19.cloned.1.call-update) | async-done | bytes 2097168 | tf_op jit(solution)/shard_map/all_gather | solution.py:58
  464.4 36.8 %all-gather.21.cloned.1.call-done = f32[16,32768]{1,0:T(8,128)} async-done(((f32[16,2048]{1,0:T(8,128)}), f32[16,32768]{1,0:T(8,128)}) %all-gather.21.cloned.1.call-update) | async-done | bytes 2097168 | tf_op jit(solution)/shard_map/all_gather | solution.py:57
  501.2 3.3 copy.124
  504.5 2.2 copy.106
  506.8 410.0 %all-gather.25.cloned.1.call-done = f32[256,32768]{1,0:T(8,128)} async-done(((f32[16,32768]{1,0:T(8,128)}), f32[256,32768]{1,0:T(8,128)}) %all-gather.25.cloned.1.call-update) | async-done | bytes 33554448 | tf_op jit(solution)/shard_map/all_gather | solution.py:10
  916.8 13.0 %reduce_sum.177 = f32[16,32768]{1,0:T(8,128)} reduce(f32[16,16,32768]{2,1,0:T(8,128)} %bitcast.135, f32[]{:T(128)} %constant.46.clone.1), dimensions={0}, to_apply=%region_17.18 | reduce | flops 7864320 | bytes 35651588 | tf_op jit(solution)/shard_map/reduce_sum | solution.py:10
  929.8 3.3 copy.122
  933.2 3.1 copy.105
  936.3 4.7 bitcast_reduce_fusion
  941.1 1.6 copy.107
  943.0 1.9 fusion.11
  (119 shorter events, 28.4 us)
Async XLA Ops:
  7.2 272.0 %copy-start = (f32[256,1024]{1,0:T(8,128)S(1)}, f32[256,1024]{1,0:T(8,128)}, u32[]{:S(2)}) copy-start(f32[256,1024]{1,0:T(8,128)} %param.24) | copy-start | bytes 3145732
  7.2 6.9 copy-start.3
  7.2 6.7 copy-start.5
  7.2 8.5 copy-start.16
  7.2 9.3 copy-start.14
  7.2 95.2 %all-gather.11.cloned.1.call-start = ((), (), s32[]{:S(2)}) async-start(), calls=%async_computation | async-start | bytes 2228224 | tf_op jit(solution)/shard_map/all_gather | solution.py:107
  13.1 174.6 %all-gather.13.cloned.1.call-start = ((), (), s32[]{:S(2)}) async-start(), calls=%async_computation.1 | async-start | bytes 2228224 | tf_op jit(solution)/shard_map/all_gather | solution.py:108
  13.9 217.6 %all-gather.15.cloned.1.call-start = ((), (), s32[]{:S(2)}) async-start(), calls=%async_computation.2 | async-start | bytes 2228224 | tf_op jit(solution)/shard_map/all_gather | solution.py:139
  194.2 3.2 copy-start.8
  198.6 71.6 %all-gather.17.cloned.1.call-start = ((), (), s32[]{:S(2)}) async-start(), calls=%async_computation.3 | async-start | bytes 2228224 | tf_op jit(solution)/shard_map/all_gather | solution.py:142
  199.2 210.9 %all-gather.23.cloned.1.call-start = ((), (), s32[]{:S(2)}) async-start(), calls=%async_computation.6 | async-start | bytes 4456448 | tf_op jit(solution)/shard_map/all_gather | solution.py:10
  236.6 0.8 copy-start.2
  276.6 1.9 copy-start.11
  276.7 2.5 copy-start.13
  276.8 3.1 copy-start.7
  279.0 1.9 copy-start.12
  280.6 131.9 %copy-start.6 = (f32[8,16,256]{2,1,0:T(8,128)}, f32[8,16,256]{2,1,0:T(8,128)S(1)}, u32[]{:S(2)}) copy-start(f32[8,16,256]{2,1,0:T(8,128)S(1)} %get-tuple-element.26) | copy-start | bytes 393220
  310.5 152.5 %all-gather.19.cloned.1.call-start = ((), (), s32[]{:S(2)}) async-start(), calls=%async_computation.4 | async-start | bytes 2228224 | tf_op jit(solution)/shard_map/all_gather | solution.py:58
  423.4 3.8 copy-start.9
  423.4 5.1 copy-start.15
  427.2 1.3 copy-start.10
  429.3 35.1 %copy-start.4 = (f32[16,16,640]{2,1,0:T(8,128)}, f32[16,16,640]{2,1,0:T(8,128)S(1)}, u32[]{:S(2)}) copy-start(f32[16,16,640]{2,1,0:T(8,128)S(1)} %fusion.28) | copy-start | bytes 1966084
  430.2 71.0 %all-gather.21.cloned.1.call-start = ((), (), s32[]{:S(2)}) async-start(), calls=%async_computation.5 | async-start | bytes 2228224 | tf_op jit(solution)/shard_map/all_gather | solution.py:57
  431.0 485.8 %all-gather.25.cloned.1.call-start = ((), (), s32[]{:S(2)}) async-start(), calls=%async_computation.7 | async-start | bytes 35651584 | tf_op jit(solution)/shard_map/all_gather | solution.py:10
  936.3 6.7 copy-start.17
  936.3 6.7 copy-start.18
  936.3 8.6 copy-start.1
Sparse Core Ops, SparseCore 0:
  13.3 89.1 all-gather.10
  105.6 82.0 all-gather.12
  198.7 32.7 all-gather.14
  233.7 36.3 all-gather.16
  310.6 99.4 all-gather.22
  430.3 32.5 all-gather.18
  464.8 36.3 all-gather.20
  503.8 412.9 all-gather.24
